TPU v7x, 128 devices: a whole 4x4x4 slice. The times are simulated.
128 devices in a mesh: rows: 32 (over y, z_lo, x), tm: 4 (over z_hi, core).
Axes of the slice: x: 4, y: 4, z: 4 (z_hi: 2, z_lo: 2; z = z_hi * 2 + z_lo), core: 2. Of those that a mesh axis runs over, the one named last changes fastest.
Arguments:
- raw_frames: bfloat16 [320, 256, 2048], P('tm', 'rows'), may hold values from -6 to 6
- dark_frame: float32 [256, 2048], P('rows'), may hold values from -0.5 to 0.5
- flat_field: float32 [256, 2048], P('rows'), may hold values from 0.5 to 1.5
- pixel_gain: float32 [256, 2048], P('rows'), may hold values from 0.1 to 1.9
- smoothing_kernel: float32 [5, 5], replicated, may hold values from 0.05 to 0.5
- bin_labels: int32 [256, 2048], P('rows'), may hold values from 0 to 71999
- lag_list: int32 [64], replicated, may hold values from 1 to 79, as said below
Outputs:
- correlation: float32 [4608000], P(('rows', 'tm'))
Inputs may be any that keep to these rules, and one draw needn't show every extreme that they name: `lag_list`: 64 distinct lags in rising order; the first is 1 and the last 79.
All inputs are finite; a program needn't handle non-finite values.
Results may differ from a plain program's by a relative error of at most 0.0054.
Values may be sent and summed in bfloat16 or wider, within the bound.
A program may use at most 256 MiB of HBM per device.

v0:
```python
import jax
import jax.numpy as jnp
from jax import lax
from jax.sharding import PartitionSpec as P

ANG = 360
QB = 200


def padded_2(array, sides, width):
    for axis, dim in sides:
        peers, length = (lax.axis_size(axis), array.shape[dim])
        up = [(i, (i + 1) % peers) for i in range(peers - 1)]
        down = [(j, i) for i, j in up]
        last = lax.slice_in_dim(array, length - width, length, axis=dim)
        initial = lax.slice_in_dim(array, 0, width, axis=dim)
        before = lax.ppermute(last, axis, up)
        after = lax.ppermute(initial, axis, down)
        array = jnp.concatenate([before, array, after], axis=dim)
    return array


def shift_columns(values, offset):
    if offset == 0:
        return values
    zero_pad = jnp.zeros(values.shape[:-1] + (abs(offset),), values.dtype)
    if offset > 0:
        return jnp.concatenate([values[..., offset:], zero_pad], axis=-1)
    return jnp.concatenate([zero_pad, values[..., :offset]], axis=-1)


def smooth_rows(padded, kernel, row_count):
    running = jnp.zeros((padded.shape[0], row_count, padded.shape[2]), jnp.float32)
    for kernel_row in range(5):
        band_rows = padded[:, kernel_row : kernel_row + row_count, :].astype(jnp.float32)
        for kernel_col in range(5):
            running = running + kernel[kernel_row, kernel_col] * shift_columns(
                band_rows, kernel_col - 2
            )
    return running.astype(jnp.bfloat16)


def lag_sums(series, extended, lag_list, divisor):
    frame_span = series.shape[0]
    lag_groups = lag_list.reshape(-1, 8)

    def one_group(lag_group):
        lag_rows = []
        for position in range(8):
            window = lax.dynamic_slice_in_dim(extended, lag_group[position], frame_span, 0)
            lag_rows.append(
                jnp.sum(series.astype(jnp.float32) * window.astype(jnp.float32), axis=0)
            )
        return jnp.stack(lag_rows)

    lagged = lax.map(one_group, lag_groups)
    return lagged.reshape(lag_list.shape[0], -1) / divisor[:, None]


def per_device(
    raw_frames, dark_frame, flat_field, pixel_gain, smoothing_kernel, bin_labels, lag_list
):
    weighted = ((raw_frames.astype(jnp.float32) - dark_frame) * flat_field * pixel_gain).astype(
        jnp.bfloat16
    )
    padded = padded_2(weighted, (("rows", 1),), 2)
    smoothed = smooth_rows(padded, smoothing_kernel, weighted.shape[1])
    block_frames = smoothed.shape[0]
    tm_count = lax.axis_size("tm")
    frame_total = block_frames * tm_count
    divisor = frame_total - lag_list.astype(jnp.float32)
    lag_count = lag_list.shape[0]
    series = lax.all_to_all(smoothed, "tm", split_axis=2, concat_axis=0, tiled=True)
    quarter = series.shape[2]
    labels_here = lax.dynamic_slice_in_dim(bin_labels, lax.axis_index("tm") * quarter, quarter, 1)
    flat_series = series.reshape(series.shape[0], -1)
    tail_zeros = jnp.zeros((block_frames, flat_series.shape[1]), jnp.bfloat16)
    extended = jnp.concatenate([flat_series, tail_zeros], 0)
    lagged = lag_sums(flat_series, extended, lag_list, divisor)
    bin_table = jnp.zeros((lag_count, ANG * QB), jnp.float32)
    bin_table = bin_table.at[:, labels_here.reshape(-1)].add(lagged.reshape(lag_count, -1))
    owned = lax.psum_scatter(bin_table.reshape(-1), ("rows", "tm"), scatter_dimension=0, tiled=True)
    return owned


def solution(mesh):
    return jax.shard_map(
        per_device,
        mesh=mesh,
        in_specs=(
            P("tm", "rows", None),
            P("rows", None),
            P("rows", None),
            P("rows", None),
            P(),
            P("rows", None),
            P(),
        ),
        out_specs=P(("rows", "tm")),
        check_vma=False,
    )
```

profile of v0, /device:TPU:1, one launch (start us, length us, event | category | flops | bytes accessed | tf_op | source)
XLA Modules:
  0.0 744.5 jit_solution(3258186887334234050)
XLA Ops:
  15.5 5.3 fusion.27
  22.3 5.4 fusion.28
  36.1 15.6 %fusion.18 = (f32[80,8,2046]{2,0,1:T(8,128)}, f32[80,8,2046]{2,0,1:T(8,128)}, f32[80,8,2046]{2,0,1:T(8,128)}, f32[80,8,2046]{2,0,1:T(8,128)}) fusion(f32[80,8,2048]{2,0,1:T(8,128)} %get-tuple-element.75, f32[80,8,2048]{2,0,1:T(8,128)} %get-tuple-element.76), kind=kLoop, calls=%fused_computation.41 | loop fusion | bytes 41902080 | tf_op jit(solution)/shard_map/slice | solution.py:29
  51.7 15.7 %fusion.19 = (f32[80,8,2047]{2,0,1:T(8,128)}, f32[80,8,2047]{2,0,1:T(8,128)}, f32[80,8,2047]{2,0,1:T(8,128)}, f32[80,8,2047]{2,0,1:T(8,128)}) fusion(f32[80,8,2048]{2,0,1:T(8,128)} %get-tuple-element.75, f32[80,8,2048]{2,0,1:T(8,128)} %get-tuple-element.76), kind=kLoop, calls=%fused_computation.42 | loop fusion | bytes 41922560 | tf_op jit(solution)/shard_map/slice | solution.py:29
  67.4 8.5 %fusion.23 = (f32[80,8,2047]{2,0,1:T(8,128)}, f32[80,8,2047]{2,0,1:T(8,128)}, f32[80,8,2047]{2,0,1:T(8,128)}, f32[80,8,2047]{2,0,1:T(8,128)}) fusion(f32[80,8,2048]{2,0,1:T(8,128)S(1)} %get-tuple-element.80, f32[80,8,2048]{2,0,1:T(8,128)S(1)} %get-tuple-element.79), kind=kLoop, calls=%fused_computation.46 | loop fusion | bytes 41922560 | tf_op jit(solution)/shard_map/slice | solution.py:29
  75.9 8.5 %fusion.22 = (f32[80,8,2046]{2,0,1:T(8,128)}, f32[80,8,2046]{2,0,1:T(8,128)}, f32[80,8,2046]{2,0,1:T(8,128)}, f32[80,8,2046]{2,0,1:T(8,128)}) fusion(f32[80,8,2048]{2,0,1:T(8,128)S(1)} %get-tuple-element.80, f32[80,8,2048]{2,0,1:T(8,128)S(1)} %get-tuple-element.79), kind=kLoop, calls=%fused_computation.45 | loop fusion | bytes 41902080 | tf_op jit(solution)/shard_map/slice | solution.py:29
  84.4 50.3 %add_convert_fusion = bf16[80,8,2048]{2,0,1:T(8,128)(2,1)} fusion(f32[80,8,2046]{2,0,1:T(8,128)} %get-tuple-element.116, f32[80,8,2047]{2,0,1:T(8,128)} %get-tuple-element.118, f32[80,8,2047]{2,0,1:T(8,128)} %get-tuple-element.119, f32[80,8,2046]{2,0,1:T(8,128)} %get-tuple-element.117, f32[80,8,2046]{2,0,1:T(8,128)} %get-tuple-element.68, ...), kind=kLoop, calls=%fused_computation.21 | loop fusion | flops 77332480 | bytes 111334496 | tf_op jit(solution)/shard_map/convert_element_type | solution.py:40
  134.6 6.2 copy.24
  140.9 7.1 all-to-all-start
  149.3 47.4 %all-to-all-done = bf16[80,8,2048]{0,1,2:T(8,128)(2,1)} async-done(((bf16[80,8,2048]{0,1,2:T(8,128)(2,1)}), bf16[80,8,2048]{0,1,2:T(8,128)(2,1)}, u32[]{:S(2)}, u32[]{:S(2)}) %all-to-all-start) | async-done | bytes 2621472 | tf_op jit(solution)/shard_map/all_to_all | solution.py:73
  196.7 6.7 copy.25
  206.1 215.6 %while.10 = (s32[]{:T(128)}, f32[8,8,4096]{2,1,0:T(8,128)}, bf16[320,4096]{1,0:T(8,128)(2,1)}, s32[8,8]{1,0:T(8,128)}, bf16[400,4096]{1,0:T(8,128)(2,1)S(1)}, /*index=5*/s32[]{:T(128)}, s32[]{:T(128)}, s32[]{:T(128)}) while((s32[]{:T(128)}, f32[8,8,4096]{2,1,0:T(8,128)}, bf16[320,4096]{1,0:T(8,128)(2,1)}, s32[8,8]{1,0:T(8,128)}, ...), condition=%wide.region_9.10_spmd, body=%wide.region_0.9_spmd.sunk | while | flops 32735256 | bytes 24249352 | solution.py:56
  223.0 9.2 %fusion.34 = (f32[4096]{0:T(1024)S(1)}, f32[4096]{0:T(1024)S(1)}, f32[4096]{0:T(1024)S(1)}, f32[4096]{0:T(1024)S(1)}, f32[4096]{0:T(1024)S(1)}, /*index=5*/f32[4096]{0:T(1024)S(1)}, f32[4096]{0:T(1024)S(1)}, f32[4096]{0:T(1024)S(1)}) fusion(bf16[320,4096]{1,0:T(8,128)(2,1)} %get-tuple-element.201, bf16[400,4096]{1,0:T(8,128)(2,1)S(1)} %get-tuple-element.203, ...), kind=kLoop, calls=%fused_computation.16.clone.1 | loop fusion | flops 32735232 | bytes 23724064 | tf_op jit(solution)/shard_map/while/body/eval_jaxpr/reduce_sum | solution.py:52
  250.0 9.2 %fusion.34 = (f32[4096]{0:T(1024)S(1)}, f32[4096]{0:T(1024)S(1)}, f32[4096]{0:T(1024)S(1)}, f32[4096]{0:T(1024)S(1)}, f32[4096]{0:T(1024)S(1)}, /*index=5*/f32[4096]{0:T(1024)S(1)}, f32[4096]{0:T(1024)S(1)}, f32[4096]{0:T(1024)S(1)}) fusion(bf16[320,4096]{1,0:T(8,128)(2,1)} %get-tuple-element.201, bf16[400,4096]{1,0:T(8,128)(2,1)S(1)} %get-tuple-element.203, ...), kind=kLoop, calls=%fused_computation.16.clone.1 | loop fusion | flops 32735232 | bytes 23724064 | tf_op jit(solution)/shard_map/while/body/eval_jaxpr/reduce_sum | solution.py:52
  276.9 9.2 %fusion.34 = (f32[4096]{0:T(1024)S(1)}, f32[4096]{0:T(1024)S(1)}, f32[4096]{0:T(1024)S(1)}, f32[4096]{0:T(1024)S(1)}, f32[4096]{0:T(1024)S(1)}, /*index=5*/f32[4096]{0:T(1024)S(1)}, f32[4096]{0:T(1024)S(1)}, f32[4096]{0:T(1024)S(1)}) fusion(bf16[320,4096]{1,0:T(8,128)(2,1)} %get-tuple-element.201, bf16[400,4096]{1,0:T(8,128)(2,1)S(1)} %get-tuple-element.203, ...), kind=kLoop, calls=%fused_computation.16.clone.1 | loop fusion | flops 32735232 | bytes 23724064 | tf_op jit(solution)/shard_map/while/body/eval_jaxpr/reduce_sum | solution.py:52
  303.8 9.2 %fusion.34 = (f32[4096]{0:T(1024)S(1)}, f32[4096]{0:T(1024)S(1)}, f32[4096]{0:T(1024)S(1)}, f32[4096]{0:T(1024)S(1)}, f32[4096]{0:T(1024)S(1)}, /*index=5*/f32[4096]{0:T(1024)S(1)}, f32[4096]{0:T(1024)S(1)}, f32[4096]{0:T(1024)S(1)}) fusion(bf16[320,4096]{1,0:T(8,128)(2,1)} %get-tuple-element.201, bf16[400,4096]{1,0:T(8,128)(2,1)S(1)} %get-tuple-element.203, ...), kind=kLoop, calls=%fused_computation.16.clone.1 | loop fusion | flops 32735232 | bytes 23724064 | tf_op jit(solution)/shard_map/while/body/eval_jaxpr/reduce_sum | solution.py:52
  330.8 9.2 %fusion.34 = (f32[4096]{0:T(1024)S(1)}, f32[4096]{0:T(1024)S(1)}, f32[4096]{0:T(1024)S(1)}, f32[4096]{0:T(1024)S(1)}, f32[4096]{0:T(1024)S(1)}, /*index=5*/f32[4096]{0:T(1024)S(1)}, f32[4096]{0:T(1024)S(1)}, f32[4096]{0:T(1024)S(1)}) fusion(bf16[320,4096]{1,0:T(8,128)(2,1)} %get-tuple-element.201, bf16[400,4096]{1,0:T(8,128)(2,1)S(1)} %get-tuple-element.203, ...), kind=kLoop, calls=%fused_computation.16.clone.1 | loop fusion | flops 32735232 | bytes 23724064 | tf_op jit(solution)/shard_map/while/body/eval_jaxpr/reduce_sum | solution.py:52
  357.7 9.2 %fusion.34 = (f32[4096]{0:T(1024)S(1)}, f32[4096]{0:T(1024)S(1)}, f32[4096]{0:T(1024)S(1)}, f32[4096]{0:T(1024)S(1)}, f32[4096]{0:T(1024)S(1)}, /*index=5*/f32[4096]{0:T(1024)S(1)}, f32[4096]{0:T(1024)S(1)}, f32[4096]{0:T(1024)S(1)}) fusion(bf16[320,4096]{1,0:T(8,128)(2,1)} %get-tuple-element.201, bf16[400,4096]{1,0:T(8,128)(2,1)S(1)} %get-tuple-element.203, ...), kind=kLoop, calls=%fused_computation.16.clone.1 | loop fusion | flops 32735232 | bytes 23724064 | tf_op jit(solution)/shard_map/while/body/eval_jaxpr/reduce_sum | solution.py:52
  384.7 9.2 %fusion.34 = (f32[4096]{0:T(1024)S(1)}, f32[4096]{0:T(1024)S(1)}, f32[4096]{0:T(1024)S(1)}, f32[4096]{0:T(1024)S(1)}, f32[4096]{0:T(1024)S(1)}, /*index=5*/f32[4096]{0:T(1024)S(1)}, f32[4096]{0:T(1024)S(1)}, f32[4096]{0:T(1024)S(1)}) fusion(bf16[320,4096]{1,0:T(8,128)(2,1)} %get-tuple-element.201, bf16[400,4096]{1,0:T(8,128)(2,1)S(1)} %get-tuple-element.203, ...), kind=kLoop, calls=%fused_computation.16.clone.1 | loop fusion | flops 32735232 | bytes 23724064 | tf_op jit(solution)/shard_map/while/body/eval_jaxpr/reduce_sum | solution.py:52
  411.6 9.2 %fusion.34 = (f32[4096]{0:T(1024)S(1)}, f32[4096]{0:T(1024)S(1)}, f32[4096]{0:T(1024)S(1)}, f32[4096]{0:T(1024)S(1)}, f32[4096]{0:T(1024)S(1)}, /*index=5*/f32[4096]{0:T(1024)S(1)}, f32[4096]{0:T(1024)S(1)}, f32[4096]{0:T(1024)S(1)}) fusion(bf16[320,4096]{1,0:T(8,128)(2,1)} %get-tuple-element.201, bf16[400,4096]{1,0:T(8,128)(2,1)S(1)} %get-tuple-element.203, ...), kind=kLoop, calls=%fused_computation.16.clone.1 | loop fusion | flops 32735232 | bytes 23724064 | tf_op jit(solution)/shard_map/while/body/eval_jaxpr/reduce_sum | solution.py:52
  423.6 36.8 %scatter_custom_fusion = f32[64,72000]{0,1:T(8,128)} fusion(s32[4096]{0:T(1024)S(1)} %bitcast.107, f32[4096,64]{1,0:T(8,128)S(1)} %copy.26, f32[]{:T(128)} %constant.3.clone.1), kind=kCustom, calls=%fused_computation.19 | custom fusion | flops 262144 | bytes 18432004 | tf_op jit(solution)/shard_map/scatter-add | solution.py:81
  460.5 27.3 %copy.27 = f32[64,72000]{1,0:T(8,128)} copy(f32[64,72000]{0,1:T(8,128)} %scatter_custom_fusion) | data formatting | bytes 36864000 | tf_op jit(solution)/shard_map/scatter-add | solution.py:81
  487.8 26.6 %reshape.68 = f32[4608000]{0:T(1024)} reshape(f32[64,72000]{1,0:T(8,128)} %copy.27) | data formatting | bytes 36864000 | tf_op jit(solution)/shard_map/reshape | solution.py:82
  514.4 221.5 %all-reduce.24.cloned.1.call-done = f32[4608000]{0:T(1024)} async-done(((f32[4608000]{0:T(1024)}), f32[4608000]{0:T(1024)}) %all-reduce.24.cloned.1.call-update) | async-done | bytes 18432016
  (66 shorter events, 44.3 us)
Async XLA Ops:
  6.5 142.1 %copy-start = (s32[8,2048]{1,0:T(8,128)S(1)}, s32[8,2048]{1,0:T(8,128)}, u32[]{:S(2)}) copy-start(s32[8,2048]{1,0:T(8,128)} %param.14) | copy-start | bytes 196612
  10.2 17.4 %collective-permute-start = (bf16[80,2,2048]{2,0,1:T(8,128)(2,1)S(1)}, bf16[80,2,2048]{2,0,1:T(8,128)(2,1)S(1)}, u32[]{:S(2)}, u32[]{:S(2)}) collective-permute-start(bf16[80,2,2048]{2,0,1:T(8,128)(2,1)S(1)} %get-tuple-element.81), channel_id=1, source_target_pairs={{0,4},{4,8},{8,12},{12,16},{16,20},{20,24},{24,28},{28,32},{32,36}... | collective-permute-start | bytes 1966088 | tf_op jit(solution)/shard_map/ppermute | solution.py:17
  14.2 6.7 copy-start.4
  14.2 17.2 %collective-permute-start.1 = (bf16[80,2,2048]{2,0,1:T(8,128)(2,1)S(1)}, bf16[80,2,2048]{2,0,1:T(8,128)(2,1)S(1)}, u32[]{:S(2)}, u32[]{:S(2)}) collective-permute-start(bf16[80,2,2048]{2,0,1:T(8,128)(2,1)S(1)} %get-tuple-element.82), channel_id=1, source_target_pairs={{4,0},{8,4},{12,8},{16,12},{20,16},{24,20},{28,24},{32,28},{36,32}... | collective-permute-start | bytes 1966088 | tf_op jit(solution)/shard_map/ppermute | solution.py:18
  31.5 4.6 copy-start.3
  140.9 7.1 copy-start.5
  140.9 55.8 %all-to-all-start = ((bf16[80,8,2048]{0,1,2:T(8,128)(2,1)}), bf16[80,8,2048]{0,1,2:T(8,128)(2,1)}, u32[]{:S(2)}, u32[]{:S(2)}) async-start(bf16[80,8,2048]{0,1,2:T(8,128)(2,1)} %copy.24), calls=%async_computation | async-start | bytes 8388608 | tf_op jit(solution)/shard_map/all_to_all | solution.py:73
  148.0 588.0 %all-reduce.24.cloned.1.call-start = ((), (), s32[]{:S(2)}) async-start(), calls=%async_computation.1 | async-start | bytes 36864000
  204.6 1.5 copy-start.2
  514.4 223.2 %copy-start.1 = (s32[8,2048]{1,0:T(8,128)S(1)}, s32[8,2048]{1,0:T(8,128)}, u32[]{:S(2)}) copy-start(s32[8,2048]{1,0:T(8,128)} %param.14) | copy-start | bytes 196612
Sparse Core Ops, SparseCore 0:
  514.6 221.3 all-reduce.23
where the time goes:
time: 748 us; the launch traced here: 744 us
  waiting for transfers between devices  273 us (36%)
  other arithmetic  170 us (23%)
  local copies, waits for them, and re-layouts  151 us (20%)
  loops' own time  124 us (17%)
  between operations  13.5 us (2%)
  starting transfers between devices  12.4 us (2%)
    unnamed x2, waiting for transfers between devices  222 us
    another operation x1, loops' own time, lag_sums(): lagged = lax.map(one_group, lag_groups)  124 us
    reduce_sum x8, other arithmetic, one_group(): jnp.sum(series.astype(jnp.float32) * window.astype(jnp.float32), axis=0)  73.2 us
    slice x6, local copies, waits for them, and re-layouts, shift_columns(): return jnp.concatenate([zero_pad, values[..., :offset]], axis=-1)  59 us
    convert_element_type x1, other arithmetic, smooth_rows(): return running.astype(jnp.bfloat16)  50.3 us
    all_to_all x1, waiting for transfers between devices, per_device(): lax.all_to_all(smoothed, 'tm', split_axis=2, concat_axis=0, tiled=True)  47.4 us
    scatter-add x1, other arithmetic, per_device(): bin_table.at[:, labels_here.reshape(-1)].add(lagged.reshape(lag_count, -1))  36.8 us
    scatter-add x1, local copies, waits for them, and re-layouts, per_device(): bin_table.at[:, labels_here.reshape(-1)].add(lagged.reshape(lag_count, -1))  27.3 us
  transfers between devices with their start and end apart: 4, of which 3 were waited for; matrix products, arithmetic and copies ran while one was open for 2% of the time, Pallas kernels for 0%

commit v1 on v0

--- a/solution.py
+++ b/solution.py
@@ -70,7 +70,10 @@
     frame_total = block_frames * tm_count
     divisor = frame_total - lag_list.astype(jnp.float32)
     lag_count = lag_list.shape[0]
-    series = lax.all_to_all(smoothed, "tm", split_axis=2, concat_axis=0, tiled=True)
+    series = jnp.concatenate(
+        lax.all_to_all(jnp.stack(jnp.split(smoothed, lax.axis_size("tm"), axis=2)), "tm", 0, 0),
+        axis=0,
+    )
     quarter = series.shape[2]
     labels_here = lax.dynamic_slice_in_dim(bin_labels, lax.axis_index("tm") * quarter, quarter, 1)
     flat_series = series.reshape(series.shape[0], -1)

time: 748 us -> 718 us (0.960)
  waiting for transfers between devices: 273 us -> 256 us
  local copies, waits for them, and re-layouts: 151 us -> 141 us
    all_to_all x1, waiting for transfers between devices: 47.4 us -> 30.6 us  [per_device(): lax.all_to_all(jnp.stack(jnp.split(smoothed, lax.axis_size('tm'), axis=2)...]
where the time goes in v1:
time: 718 us; the launch traced here: 715 us
  waiting for transfers between devices  256 us (36%)
  other arithmetic  172 us (24%)
  local copies, waits for them, and re-layouts  141 us (20%)
  loops' own time  120 us (17%)
  between operations  13.5 us (2%)
  starting transfers between devices  12.2 us (2%)
    unnamed x2, waiting for transfers between devices  221 us
    another operation x1, loops' own time, lag_sums(): lagged = lax.map(one_group, lag_groups)  120 us
    reduce_sum x8, other arithmetic, one_group(): jnp.sum(series.astype(jnp.float32) * window.astype(jnp.float32), axis=0)  73.2 us
    slice x6, local copies, waits for them, and re-layouts, shift_columns(): return jnp.concatenate([zero_pad, values[..., :offset]], axis=-1)  59 us
    convert_element_type x1, other arithmetic, smooth_rows(): return running.astype(jnp.bfloat16)  50.3 us
    scatter-add x1, other arithmetic, per_device(): bin_table.at[:, labels_here.reshape(-1)].add(lagged.reshape(lag_count, -1))  36.8 us
    all_to_all x1, waiting for transfers between devices, per_device(): lax.all_to_all(jnp.stack(jnp.split(smoothed, lax.axis_size('tm'), axis=2)...  30.6 us
    scatter-add x1, local copies, waits for them, and re-layouts, per_device(): bin_table.at[:, labels_here.reshape(-1)].add(lagged.reshape(lag_count, -1))  27.3 us
  transfers between devices with their start and end apart: 4, of which 3 were waited for; matrix products, arithmetic and copies ran while one was open for 2% of the time, Pallas kernels for 0%

profile of v1, /device:TPU:1, one launch (start us, length us, event | category | flops | bytes accessed | tf_op | source)
XLA Modules:
  0.0 714.6 jit_solution(4539091246216077780)
XLA Ops:
  10.2 4.0 collective-permute-start
  15.5 5.3 fusion.27
  22.3 5.4 fusion.28
  31.5 4.6 fusion.13
  36.1 15.6 %fusion.18 = (f32[80,8,2046]{2,0,1:T(8,128)}, f32[80,8,2046]{2,0,1:T(8,128)}, f32[80,8,2046]{2,0,1:T(8,128)}, f32[80,8,2046]{2,0,1:T(8,128)}) fusion(f32[80,8,2048]{2,0,1:T(8,128)} %get-tuple-element.75, f32[80,8,2048]{2,0,1:T(8,128)} %get-tuple-element.76), kind=kLoop, calls=%fused_computation.46 | loop fusion | bytes 41902080 | tf_op jit(solution)/shard_map/slice | solution.py:29
  51.7 15.7 %fusion.19 = (f32[80,8,2047]{2,0,1:T(8,128)}, f32[80,8,2047]{2,0,1:T(8,128)}, f32[80,8,2047]{2,0,1:T(8,128)}, f32[80,8,2047]{2,0,1:T(8,128)}) fusion(f32[80,8,2048]{2,0,1:T(8,128)} %get-tuple-element.75, f32[80,8,2048]{2,0,1:T(8,128)} %get-tuple-element.76), kind=kLoop, calls=%fused_computation.47 | loop fusion | bytes 41922560 | tf_op jit(solution)/shard_map/slice | solution.py:29
  67.4 8.5 %fusion.23 = (f32[80,8,2047]{2,0,1:T(8,128)}, f32[80,8,2047]{2,0,1:T(8,128)}, f32[80,8,2047]{2,0,1:T(8,128)}, f32[80,8,2047]{2,0,1:T(8,128)}) fusion(f32[80,8,2048]{2,0,1:T(8,128)S(1)} %get-tuple-element.84, f32[80,8,2048]{2,0,1:T(8,128)S(1)} %get-tuple-element.83), kind=kLoop, calls=%fused_computation.51 | loop fusion | bytes 41922560 | tf_op jit(solution)/shard_map/slice | solution.py:29
  75.9 8.5 %fusion.22 = (f32[80,8,2046]{2,0,1:T(8,128)}, f32[80,8,2046]{2,0,1:T(8,128)}, f32[80,8,2046]{2,0,1:T(8,128)}, f32[80,8,2046]{2,0,1:T(8,128)}) fusion(f32[80,8,2048]{2,0,1:T(8,128)S(1)} %get-tuple-element.84, f32[80,8,2048]{2,0,1:T(8,128)S(1)} %get-tuple-element.83), kind=kLoop, calls=%fused_computation.50 | loop fusion | bytes 41902080 | tf_op jit(solution)/shard_map/slice | solution.py:29
  84.4 50.3 %add_convert_fusion = bf16[80,8,2048]{2,0,1:T(8,128)(2,1)} fusion(f32[80,8,2046]{2,0,1:T(8,128)} %get-tuple-element.120, f32[80,8,2047]{2,0,1:T(8,128)} %get-tuple-element.122, f32[80,8,2047]{2,0,1:T(8,128)} %get-tuple-element.123, f32[80,8,2046]{2,0,1:T(8,128)} %get-tuple-element.121, f32[80,8,2046]{2,0,1:T(8,128)} %get-tuple-element.68, ...), kind=kLoop, calls=%fused_computation.21 | loop fusion | flops 77332480 | bytes 111334496 | tf_op jit(solution)/shard_map/convert_element_type | solution.py:40
  138.3 7.0 all-to-all-start
  146.5 30.6 %all-to-all-done = bf16[4,80,8,512]{3,1,2,0:T(8,128)(2,1)S(1)} async-done(((bf16[4,80,8,512]{3,1,2,0:T(8,128)(2,1)}), bf16[4,80,8,512]{3,1,2,0:T(8,128)(2,1)S(1)}, u32[]{:S(2)}, u32[]{:S(2)}) %all-to-all-start) | async-done | bytes 2621472 | tf_op jit(solution)/shard_map/all_to_all | solution.py:74
  181.3 210.8 %while.10 = (s32[]{:T(128)}, f32[8,8,4096]{2,1,0:T(8,128)}, bf16[320,4096]{1,0:T(8,128)(2,1)}, s32[8,8]{1,0:T(8,128)}, bf16[400,4096]{1,0:T(8,128)(2,1)S(1)}, /*index=5*/s32[]{:T(128)}, s32[]{:T(128)}, s32[]{:T(128)}) while((s32[]{:T(128)}, f32[8,8,4096]{2,1,0:T(8,128)}, bf16[320,4096]{1,0:T(8,128)(2,1)}, s32[8,8]{1,0:T(8,128)}, ...), condition=%wide.region_9.10_spmd, body=%wide.region_0.9_spmd.sunk | while | flops 32735256 | bytes 24249352 | solution.py:56
  197.6 9.2 %fusion.34 = (f32[4096]{0:T(1024)S(1)}, f32[4096]{0:T(1024)S(1)}, f32[4096]{0:T(1024)S(1)}, f32[4096]{0:T(1024)S(1)}, f32[4096]{0:T(1024)S(1)}, /*index=5*/f32[4096]{0:T(1024)S(1)}, f32[4096]{0:T(1024)S(1)}, f32[4096]{0:T(1024)S(1)}) fusion(bf16[320,4096]{1,0:T(8,128)(2,1)} %get-tuple-element.205, bf16[400,4096]{1,0:T(8,128)(2,1)S(1)} %get-tuple-element.207, ...), kind=kLoop, calls=%fused_computation.16.clone.1 | loop fusion | flops 32735232 | bytes 23724064 | tf_op jit(solution)/shard_map/while/body/eval_jaxpr/reduce_sum | solution.py:52
  224.0 9.2 %fusion.34 = (f32[4096]{0:T(1024)S(1)}, f32[4096]{0:T(1024)S(1)}, f32[4096]{0:T(1024)S(1)}, f32[4096]{0:T(1024)S(1)}, f32[4096]{0:T(1024)S(1)}, /*index=5*/f32[4096]{0:T(1024)S(1)}, f32[4096]{0:T(1024)S(1)}, f32[4096]{0:T(1024)S(1)}) fusion(bf16[320,4096]{1,0:T(8,128)(2,1)} %get-tuple-element.205, bf16[400,4096]{1,0:T(8,128)(2,1)S(1)} %get-tuple-element.207, ...), kind=kLoop, calls=%fused_computation.16.clone.1 | loop fusion | flops 32735232 | bytes 23724064 | tf_op jit(solution)/shard_map/while/body/eval_jaxpr/reduce_sum | solution.py:52
  250.3 9.2 %fusion.34 = (f32[4096]{0:T(1024)S(1)}, f32[4096]{0:T(1024)S(1)}, f32[4096]{0:T(1024)S(1)}, f32[4096]{0:T(1024)S(1)}, f32[4096]{0:T(1024)S(1)}, /*index=5*/f32[4096]{0:T(1024)S(1)}, f32[4096]{0:T(1024)S(1)}, f32[4096]{0:T(1024)S(1)}) fusion(bf16[320,4096]{1,0:T(8,128)(2,1)} %get-tuple-element.205, bf16[400,4096]{1,0:T(8,128)(2,1)S(1)} %get-tuple-element.207, ...), kind=kLoop, calls=%fused_computation.16.clone.1 | loop fusion | flops 32735232 | bytes 23724064 | tf_op jit(solution)/shard_map/while/body/eval_jaxpr/reduce_sum | solution.py:52
  276.7 9.2 %fusion.34 = (f32[4096]{0:T(1024)S(1)}, f32[4096]{0:T(1024)S(1)}, f32[4096]{0:T(1024)S(1)}, f32[4096]{0:T(1024)S(1)}, f32[4096]{0:T(1024)S(1)}, /*index=5*/f32[4096]{0:T(1024)S(1)}, f32[4096]{0:T(1024)S(1)}, f32[4096]{0:T(1024)S(1)}) fusion(bf16[320,4096]{1,0:T(8,128)(2,1)} %get-tuple-element.205, bf16[400,4096]{1,0:T(8,128)(2,1)S(1)} %get-tuple-element.207, ...), kind=kLoop, calls=%fused_computation.16.clone.1 | loop fusion | flops 32735232 | bytes 23724064 | tf_op jit(solution)/shard_map/while/body/eval_jaxpr/reduce_sum | solution.py:52
  303.1 9.2 %fusion.34 = (f32[4096]{0:T(1024)S(1)}, f32[4096]{0:T(1024)S(1)}, f32[4096]{0:T(1024)S(1)}, f32[4096]{0:T(1024)S(1)}, f32[4096]{0:T(1024)S(1)}, /*index=5*/f32[4096]{0:T(1024)S(1)}, f32[4096]{0:T(1024)S(1)}, f32[4096]{0:T(1024)S(1)}) fusion(bf16[320,4096]{1,0:T(8,128)(2,1)} %get-tuple-element.205, bf16[400,4096]{1,0:T(8,128)(2,1)S(1)} %get-tuple-element.207, ...), kind=kLoop, calls=%fused_computation.16.clone.1 | loop fusion | flops 32735232 | bytes 23724064 | tf_op jit(solution)/shard_map/while/body/eval_jaxpr/reduce_sum | solution.py:52
  329.4 9.2 %fusion.34 = (f32[4096]{0:T(1024)S(1)}, f32[4096]{0:T(1024)S(1)}, f32[4096]{0:T(1024)S(1)}, f32[4096]{0:T(1024)S(1)}, f32[4096]{0:T(1024)S(1)}, /*index=5*/f32[4096]{0:T(1024)S(1)}, f32[4096]{0:T(1024)S(1)}, f32[4096]{0:T(1024)S(1)}) fusion(bf16[320,4096]{1,0:T(8,128)(2,1)} %get-tuple-element.205, bf16[400,4096]{1,0:T(8,128)(2,1)S(1)} %get-tuple-element.207, ...), kind=kLoop, calls=%fused_computation.16.clone.1 | loop fusion | flops 32735232 | bytes 23724064 | tf_op jit(solution)/shard_map/while/body/eval_jaxpr/reduce_sum | solution.py:52
  355.8 9.2 %fusion.34 = (f32[4096]{0:T(1024)S(1)}, f32[4096]{0:T(1024)S(1)}, f32[4096]{0:T(1024)S(1)}, f32[4096]{0:T(1024)S(1)}, f32[4096]{0:T(1024)S(1)}, /*index=5*/f32[4096]{0:T(1024)S(1)}, f32[4096]{0:T(1024)S(1)}, f32[4096]{0:T(1024)S(1)}) fusion(bf16[320,4096]{1,0:T(8,128)(2,1)} %get-tuple-element.205, bf16[400,4096]{1,0:T(8,128)(2,1)S(1)} %get-tuple-element.207, ...), kind=kLoop, calls=%fused_computation.16.clone.1 | loop fusion | flops 32735232 | bytes 23724064 | tf_op jit(solution)/shard_map/while/body/eval_jaxpr/reduce_sum | solution.py:52
  382.1 9.2 %fusion.34 = (f32[4096]{0:T(1024)S(1)}, f32[4096]{0:T(1024)S(1)}, f32[4096]{0:T(1024)S(1)}, f32[4096]{0:T(1024)S(1)}, f32[4096]{0:T(1024)S(1)}, /*index=5*/f32[4096]{0:T(1024)S(1)}, f32[4096]{0:T(1024)S(1)}, f32[4096]{0:T(1024)S(1)}) fusion(bf16[320,4096]{1,0:T(8,128)(2,1)} %get-tuple-element.205, bf16[400,4096]{1,0:T(8,128)(2,1)S(1)} %get-tuple-element.207, ...), kind=kLoop, calls=%fused_computation.16.clone.1 | loop fusion | flops 32735232 | bytes 23724064 | tf_op jit(solution)/shard_map/while/body/eval_jaxpr/reduce_sum | solution.py:52
  394.1 36.8 %scatter_custom_fusion = f32[64,72000]{0,1:T(8,128)} fusion(s32[4096]{0:T(1024)S(1)} %bitcast.112, f32[4096,64]{1,0:T(8,128)S(1)} %copy.20, f32[]{:T(128)} %constant.3.clone.1), kind=kCustom, calls=%fused_computation.19 | custom fusion | flops 262144 | bytes 18432004 | tf_op jit(solution)/shard_map/scatter-add | solution.py:84
  430.9 27.3 %copy.21 = f32[64,72000]{1,0:T(8,128)} copy(f32[64,72000]{0,1:T(8,128)} %scatter_custom_fusion) | data formatting | bytes 36864000 | tf_op jit(solution)/shard_map/scatter-add | solution.py:84
  458.3 26.6 %reshape.63 = f32[4608000]{0:T(1024)} reshape(f32[64,72000]{1,0:T(8,128)} %copy.21) | data formatting | bytes 36864000 | tf_op jit(solution)/shard_map/reshape | solution.py:85
  484.9 221.1 %all-reduce.24.cloned.1.call-done = f32[4608000]{0:T(1024)} async-done(((f32[4608000]{0:T(1024)}), f32[4608000]{0:T(1024)}) %all-reduce.24.cloned.1.call-update) | async-done | bytes 18432016
  (67 shorter events, 40.8 us)
Async XLA Ops:
  6.5 139.4 %copy-start = (s32[8,2048]{1,0:T(8,128)S(1)}, s32[8,2048]{1,0:T(8,128)}, u32[]{:S(2)}) copy-start(s32[8,2048]{1,0:T(8,128)} %param.14) | copy-start | bytes 196612
  10.2 17.4 %collective-permute-start = (bf16[80,2,2048]{2,0,1:T(8,128)(2,1)S(1)}, bf16[80,2,2048]{2,0,1:T(8,128)(2,1)S(1)}, u32[]{:S(2)}, u32[]{:S(2)}) collective-permute-start(bf16[80,2,2048]{2,0,1:T(8,128)(2,1)S(1)} %get-tuple-element.85), channel_id=1, source_target_pairs={{0,4},{4,8},{8,12},{12,16},{16,20},{20,24},{24,28},{28,32},{32,36}... | collective-permute-start | bytes 1966088 | tf_op jit(solution)/shard_map/ppermute | solution.py:17
  14.2 6.7 copy-start.4
  14.2 17.2 %collective-permute-start.1 = (bf16[80,2,2048]{2,0,1:T(8,128)(2,1)S(1)}, bf16[80,2,2048]{2,0,1:T(8,128)(2,1)S(1)}, u32[]{:S(2)}, u32[]{:S(2)}) collective-permute-start(bf16[80,2,2048]{2,0,1:T(8,128)(2,1)S(1)} %get-tuple-element.86), channel_id=1, source_target_pairs={{4,0},{8,4},{12,8},{16,12},{20,16},{24,20},{28,24},{32,28},{36,32}... | collective-permute-start | bytes 1966088 | tf_op jit(solution)/shard_map/ppermute | solution.py:18
  31.5 4.6 copy-start.3
  136.5 8.8 %copy-start.5 = (s32[64]{0:T(128)S(1)}, s32[64]{0:T(128)}, u32[]{:S(2)}) copy-start(s32[64]{0:T(128)} %param.15) | copy-start | bytes 772
  138.3 38.8 %all-to-all-start = ((bf16[4,80,8,512]{3,1,2,0:T(8,128)(2,1)}), bf16[4,80,8,512]{3,1,2,0:T(8,128)(2,1)S(1)}, u32[]{:S(2)}, u32[]{:S(2)}) async-start(bf16[4,80,8,512]{3,1,2,0:T(8,128)(2,1)} %pad_maximum_fusion.2), calls=%async_computation | async-start | bytes 5242880 | tf_op jit(solution)/shard_map/all_to_all | solution.py:74
  145.3 560.7 %all-reduce.24.cloned.1.call-start = ((), (), s32[]{:S(2)}) async-start(), calls=%async_computation.1 | async-start | bytes 36864000
  179.8 1.5 copy-start.2
  484.9 222.8 %copy-start.1 = (s32[8,2048]{1,0:T(8,128)S(1)}, s32[8,2048]{1,0:T(8,128)}, u32[]{:S(2)}) copy-start(s32[8,2048]{1,0:T(8,128)} %param.14) | copy-start | bytes 196612
Sparse Core Ops, SparseCore 0:
  485.0 220.9 all-reduce.23
